TPU v7x, 512 devices: a whole 4x8x8 slice. The times are simulated.
512 devices in a mesh: tok: 16 (over z, core), voc: 32 (over y, x).
Axes of the slice: x: 4, y: 8, z: 8, core: 2. Of those that a mesh axis runs over, the one named last changes fastest.
Arguments:
- hidden: bfloat16 [256, 2304], P('tok', 'voc'), may hold values from -18 to 18
- head: bfloat16 [2304, 131072], P(None, ('tok', 'voc')), as said below
- targets: int32 [256], replicated, may hold values from 0 to 131071
- probe_hidden: bfloat16 [256, 2304], P('tok', 'voc'), may hold values from -6 to 6
- probe_head: bfloat16 [2304, 131072], P(None, ('tok', 'voc')), may hold values from -0.5 to 0.5
Outputs:
- head_out: float32 [2304, 131072], P(None, ('tok', 'voc'))
- hidden_out: float32 [256, 2304], P('tok', 'voc')
Inputs may be any that keep to these rules, and one draw needn't show every extreme that they name: `head`: entries lie within 66 / sqrt(2304) in magnitude.
All inputs are finite; a program needn't handle non-finite values.
Results may differ from a plain program's by a relative error of at most 0.0075.
Values may be sent and summed in bfloat16 or wider, within the bound.
A program may use at most 64 MiB of HBM per device.

v0:
```python
import jax
import jax.numpy as jnp
from jax import lax
from jax.sharding import PartitionSpec as P

softcap_value = 30.0
zloss_weight = 0.0001


def local(hidden, head, targets, probe_hidden, probe_head):
    voc_count = lax.axis_size("voc")
    vocab_width = head.shape[1]
    stacked = jnp.stack([hidden, probe_hidden])
    features = lax.all_gather(stacked, "voc", axis=2, tiled=True)
    gathered = lax.all_gather(features, "tok", axis=1, tiled=True)
    row_hidden = gathered[0]
    row_probe = gathered[1]
    logits = jnp.dot(row_hidden, head, preferred_element_type=jnp.float32)
    tangent = jnp.dot(row_probe, head, preferred_element_type=jnp.float32) + jnp.dot(
        row_hidden, probe_head, preferred_element_type=jnp.float32
    )
    capped = jnp.tanh(logits / softcap_value)
    cap_slope = 1.0 - capped * capped
    exponent = jnp.exp(softcap_value * capped)
    cap_tangent = cap_slope * tangent
    row_total = lax.psum(jnp.sum(exponent, axis=1), ("tok", "voc"))
    probability = exponent / row_total[:, None]
    mean_tangent = lax.psum(jnp.sum(probability * cap_tangent, axis=1), ("tok", "voc"))
    factor = 1.0 + 2.0 * zloss_weight * jnp.log(row_total)
    offset = (lax.axis_index("tok") * voc_count + lax.axis_index("voc")) * vocab_width
    columns = offset + lax.iota(jnp.int32, vocab_width)
    onehot = (targets[:, None] == columns[None, :]).astype(jnp.float32)
    grad_cap = factor[:, None] * probability - onehot
    grad_tan = probability * (
        factor[:, None] * (cap_tangent - mean_tangent[:, None])
        + 2.0 * zloss_weight * mean_tangent[:, None]
    )
    slope_tan = -2.0 / softcap_value * capped * cap_slope * tangent
    dlogit = (grad_cap * cap_slope).astype(jnp.bfloat16)
    dlogit_tan = (grad_tan * cap_slope + grad_cap * slope_tan).astype(jnp.bfloat16)
    head_out = jnp.einsum(
        "krd,krv->dv", gathered, jnp.stack([dlogit_tan, dlogit]), preferred_element_type=jnp.float32
    )
    probe_part = lax.dot_general(
        dlogit, probe_head, (((1,), (1,)), ((), ())), preferred_element_type=jnp.float32
    )
    head_part = lax.dot_general(
        dlogit_tan, head, (((1,), (1,)), ((), ())), preferred_element_type=jnp.float32
    )
    summed = lax.psum_scatter(probe_part + head_part, "tok", scatter_dimension=0, tiled=True)
    hidden_out = lax.psum_scatter(summed, "voc", scatter_dimension=1, tiled=True)
    return (head_out, hidden_out)


def solution(mesh):
    return jax.shard_map(
        local,
        mesh=mesh,
        in_specs=(
            P("tok", "voc"),
            P(None, ("tok", "voc")),
            P(),
            P("tok", "voc"),
            P(None, ("tok", "voc")),
        ),
        out_specs=(P(None, ("tok", "voc")), P("tok", "voc")),
        check_vma=False,
    )
```

profile of v0, /device:TPU:2, one launch (start us, length us, event | category | flops | bytes accessed | tf_op | source)
XLA Modules:
  0.0 533.8 jit_solution(17602048826722212761)
XLA Ops:
  7.2 0.0 all-gather.2.cloned.1.call-start
  7.2 0.8 pad_maximum_fusion
  8.0 0.1 copy.12
  8.1 52.7 %all_gather.6 = bf16[2,16,2304]{1,0,2:T(2,128)(2,1)S(1)} all-gather(bf16[2,16,72]{1,0,2:T(2,128)(2,1)S(1)} %copy.12), channel_id=1, replica_groups=mesh['tok'=16,'voc'=32] {'voc'}, dimensions={2}, use_global_device_ids=true | all-gather | bytes 152064 | tf_op jit(solution)/shard_map/all_gather | solution.py:14
  60.8 2.2 copy.13
  63.0 0.0 all-gather.2.cloned.1.call-update
  63.0 0.0 reduce-scatter.3.cloned.1.call-start
  63.1 0.6 iota_add_fusion
  63.7 42.7 %all-gather.2.cloned.1.call-done = bf16[2,256,2304]{2,1,0:T(8,128)(2,1)} async-done(((bf16[2,16,2304]{2,1,0:T(8,128)(2,1)}), bf16[2,256,2304]{2,1,0:T(8,128)(2,1)}) %all-gather.2.cloned.1.call-update) | async-done | bytes 2359312 | tf_op jit(solution)/shard_map/all_gather | solution.py:15
  106.4 2.7 fusion.8
  109.1 96.8 %psum.14 = f32[256]{0:T(256)S(1)} all-reduce(f32[256]{0:T(256)S(1)} %get-tuple-element.4), channel_id=1, replica_groups=mesh['tok'=16,'voc'=32] {'tok','voc'}, use_global_device_ids=true, to_apply=%region_1.0 | all-reduce | flops 256 | bytes 2048 | tf_op jit(solution)/shard_map/psum | solution.py:26
  205.8 1.9 fusion.3
  207.8 1.8 multiply_reduce_fusion
  209.6 94.9 %psum.15 = f32[256]{0:T(256)S(1)} all-reduce(f32[256]{0:T(256)} %get-tuple-element.6), channel_id=1, replica_groups=mesh['tok'=16,'voc'=32] {'tok','voc'}, use_global_device_ids=true, to_apply=%region_3.0 | all-reduce | flops 256 | bytes 2048 | tf_op jit(solution)/shard_map/psum | solution.py:28
  304.5 1.2 add_convert_fusion
  305.8 1.9 fusion.10
  307.7 2.0 convolution_add_fusion
  309.6 0.0 reduce-scatter.3.cloned.1.call-update
  309.7 0.0 all-reduce.3.cloned.1.call-start
  309.7 1.3 dynamic-slice
  311.6 58.5 %reduce-scatter.3.cloned.1.call-done = f32[16,2304]{1,0:T(8,128)} async-done(((f32[256,2304]{1,0:T(8,128)}), f32[16,2304]{1,0:T(8,128)}) %reduce-scatter.3.cloned.1.call-update) | async-done | bytes 147472 | tf_op jit(solution)/shard_map/reduce_scatter | solution.py:50
  370.1 3.2 convolution_bitcast_fusion
  373.3 152.5 %all-reduce.3.cloned.1.call-done = f32[16,2304]{1,0:T(8,128)} async-done(((f32[16,2304]{1,0:T(8,128)}), f32[16,2304]{1,0:T(8,128)}) %all-reduce.3.cloned.1.call-update) | async-done | bytes 147472
  525.9 1.4 constant_dynamic-slice_fusion
  (15 shorter events, 0.1 us)
Async XLA Ops:
  7.2 99.2 %copy-start = (bf16[2304,256]{1,0:T(8,128)(2,1)S(1)}, bf16[2304,256]{1,0:T(8,128)(2,1)}, u32[]{:S(2)}) copy-start(bf16[2304,256]{1,0:T(8,128)(2,1)} %param.6) | copy-start | bytes 3538948
  7.2 99.2 %all-gather.2.cloned.1.call-start = ((), (), s32[]{:S(2)}) async-start(), calls=%async_computation.1 | async-start | bytes 2506752 | tf_op jit(solution)/shard_map/all_gather | solution.py:15
  63.0 307.1 %reduce-scatter.3.cloned.1.call-start = ((), (), s32[]{:S(2)}) async-start(), calls=%async_computation.2 | async-start | bytes 2506752 | tf_op jit(solution)/shard_map/reduce_scatter | solution.py:50
  106.4 99.5 %copy-start.1 = (bf16[2,256,2304]{2,1,0:T(8,128)(2,1)S(1)}, bf16[2,256,2304]{2,1,0:T(8,128)(2,1)}, u32[]{:S(2)}) copy-start(bf16[2,256,2304]{2,1,0:T(8,128)(2,1)} %all-gather.2.cloned.1.call-done) | copy-start | bytes 7077892
  205.8 1.9 copy-start.4
  207.8 96.8 %copy-start.5 = (s32[256]{0:T(256)S(1)}, s32[256]{0:T(256)}, u32[]{:S(2)}) copy-start(s32[256]{0:T(256)} %param.7) | copy-start | bytes 3076
  305.7 1.9 copy-start.3
  305.8 1.9 copy-start.2
  309.7 216.2 %all-reduce.3.cloned.1.call-start = ((), (), s32[]{:S(2)}) async-start(), calls=%async_computation.3 | async-start | bytes 294912
Sparse Core Ops, SparseCore 0:
  63.1 43.1 all-gather.1
  309.8 60.2 reduce-scatter.2
  373.6 152.2 all-reduce.2
where the time goes:
time: 534 us
  waiting for transfers between devices  254 us (48%)
  blocking collectives  244 us (46%)
  between operations  14.5 us (3%)
  matrix products  13.5 us (3%)
    unnamed x4, waiting for transfers between devices  153 us
    psum x1, blocking collectives, local(): row_total = lax.psum(jnp.sum(exponent, axis=1), ('tok', 'voc'))  96.8 us
    psum x1, blocking collectives, local(): lax.psum(jnp.sum(probability * cap_tangent, axis=1), ('tok', 'voc'))  94.9 us
    reduce_scatter x1, waiting for transfers between devices, local(): lax.psum_scatter(probe_part + head_part, 'tok', scatter_dimension=0, tile...  58.5 us
    all_gather x1, blocking collectives, local(): features = lax.all_gather(stacked, 'voc', axis=2, tiled=True)  52.7 us
    all_gather x1, waiting for transfers between devices, local(): gathered = lax.all_gather(features, 'tok', axis=1, tiled=True)  42.7 us
  transfers between devices with their start and end apart: 3, of which 3 were waited for; matrix products, arithmetic and copies ran while one was open for 1% of the time, Pallas kernels for 0%

commit v1 on v0

--- a/solution.py
+++ b/solution.py
@@ -23,9 +23,13 @@
     cap_slope = 1.0 - capped * capped
     exponent = jnp.exp(softcap_value * capped)
     cap_tangent = cap_slope * tangent
-    row_total = lax.psum(jnp.sum(exponent, axis=1), ("tok", "voc"))
+    stats = lax.psum(
+        jnp.stack([jnp.sum(exponent, axis=1), jnp.sum(exponent * cap_tangent, axis=1)]),
+        ("tok", "voc"),
+    )
+    row_total = stats[0]
     probability = exponent / row_total[:, None]
-    mean_tangent = lax.psum(jnp.sum(probability * cap_tangent, axis=1), ("tok", "voc"))
+    mean_tangent = stats[1] / row_total
     factor = 1.0 + 2.0 * zloss_weight * jnp.log(row_total)
     offset = (lax.axis_index("tok") * voc_count + lax.axis_index("voc")) * vocab_width
     columns = offset + lax.iota(jnp.int32, vocab_width)

time: 534 us -> 436 us (0.82)
  blocking collectives: 244 us -> 149 us
    psum x2 -> x1, blocking collectives: 192 us -> 96.8 us  [local(): lax.psum(jnp.stack([jnp.sum(exponent, axis=1), jnp.sum(exponent * cap_tan...]
where the time goes in v1:
time: 436 us
  waiting for transfers between devices  253 us (58%)
  blocking collectives  149 us (34%)
  between operations  14.5 us (3%)
  matrix products  11.3 us (3%)
  local copies, waits for them, and re-layouts  5.01 us (1%)
    unnamed x4, waiting for transfers between devices  153 us
    psum x1, blocking collectives, local(): lax.psum(jnp.stack([jnp.sum(exponent, axis=1), jnp.sum(exponent * cap_tan...  96.8 us
    reduce_scatter x1, waiting for transfers between devices, local(): lax.psum_scatter(probe_part + head_part, 'tok', scatter_dimension=0, tile...  57.4 us
    all_gather x1, blocking collectives, local(): features = lax.all_gather(stacked, 'voc', axis=2, tiled=True)  52.7 us
    all_gather x1, waiting for transfers between devices, local(): gathered = lax.all_gather(features, 'tok', axis=1, tiled=True)  43.3 us
  transfers between devices with their start and end apart: 3, of which 3 were waited for; matrix products, arithmetic and copies ran while one was open for 1% of the time, Pallas kernels for 0%

profile of v1, /device:TPU:2, one launch (start us, length us, event | category | flops | bytes accessed | tf_op | source)
XLA Modules:
  0.0 435.7 jit_solution(9446589212632024018)
XLA Ops:
  7.2 0.0 copy-start
  7.2 0.0 all-gather.2.cloned.1.call-start
  7.2 0.8 pad_maximum_fusion
  8.0 0.1 copy.12
  8.1 52.7 %all_gather.6 = bf16[2,16,2304]{1,0,2:T(2,128)(2,1)S(1)} all-gather(bf16[2,16,72]{1,0,2:T(2,128)(2,1)S(1)} %copy.12), channel_id=1, replica_groups=mesh['tok'=16,'voc'=32] {'voc'}, dimensions={2}, use_global_device_ids=true | all-gather | bytes 152064 | tf_op jit(solution)/shard_map/all_gather | solution.py:14
  60.8 2.2 copy.13
  63.0 0.0 all-gather.2.cloned.1.call-update
  63.0 0.0 reduce-scatter.3.cloned.1.call-start
  63.1 43.3 %all-gather.2.cloned.1.call-done = bf16[2,256,2304]{2,1,0:T(8,128)(2,1)} async-done(((bf16[2,16,2304]{2,1,0:T(8,128)(2,1)}), bf16[2,256,2304]{2,1,0:T(8,128)(2,1)}) %all-gather.2.cloned.1.call-update) | async-done | bytes 2359312 | tf_op jit(solution)/shard_map/all_gather | solution.py:15
  106.4 2.4 fusion.3
  108.7 0.6 fusion.1
  109.4 1.3 fusion.9
  110.7 96.8 %psum.7 = f32[2,256]{1,0:T(2,128)S(1)} all-reduce(f32[2,256]{1,0:T(2,128)S(1)} %pad_maximum_fusion.1), channel_id=1, replica_groups=mesh['tok'=16,'voc'=32] {'tok','voc'}, use_global_device_ids=true, to_apply=%region_2.0 | all-reduce | flops 512 | bytes 4096 | tf_op jit(solution)/shard_map/psum | solution.py:26
  207.5 1.2 add_convert_fusion
  208.8 1.9 fusion.12
  210.7 2.0 convolution_add_fusion
  212.6 0.0 reduce-scatter.3.cloned.1.call-update
  212.7 0.0 all-reduce.3.cloned.1.call-start
  212.7 1.3 dynamic-slice
  214.6 57.4 %reduce-scatter.3.cloned.1.call-done = f32[16,2304]{1,0:T(8,128)} async-done(((f32[256,2304]{1,0:T(8,128)}), f32[16,2304]{1,0:T(8,128)}) %reduce-scatter.3.cloned.1.call-update) | async-done | bytes 147472 | tf_op jit(solution)/shard_map/reduce_scatter | solution.py:54
  272.0 0.0 all-reduce.3.cloned.1.call-update
  272.1 3.2 convolution_bitcast_fusion
  275.3 152.5 %all-reduce.3.cloned.1.call-done = f32[16,2304]{1,0:T(8,128)} async-done(((f32[16,2304]{1,0:T(8,128)}), f32[16,2304]{1,0:T(8,128)}) %all-reduce.3.cloned.1.call-update) | async-done | bytes 147472
  427.8 1.4 constant_dynamic-slice_fusion
  (15 shorter events, 0.1 us)
Async XLA Ops:
  7.2 101.6 %copy-start = (bf16[2304,256]{1,0:T(8,128)(2,1)S(1)}, bf16[2304,256]{1,0:T(8,128)(2,1)}, u32[]{:S(2)}) copy-start(bf16[2304,256]{1,0:T(8,128)(2,1)} %param.6) | copy-start | bytes 3538948
  7.2 99.2 %all-gather.2.cloned.1.call-start = ((), (), s32[]{:S(2)}) async-start(), calls=%async_computation.1 | async-start | bytes 2506752 | tf_op jit(solution)/shard_map/all_gather | solution.py:15
  63.0 209.0 %reduce-scatter.3.cloned.1.call-start = ((), (), s32[]{:S(2)}) async-start(), calls=%async_computation.2 | async-start | bytes 2506752 | tf_op jit(solution)/shard_map/reduce_scatter | solution.py:54
  106.4 2.4 copy-start.1
  109.3 1.3 copy-start.4
  109.4 98.1 %copy-start.5 = (s32[256]{0:T(256)S(1)}, s32[256]{0:T(256)}, u32[]{:S(2)}) copy-start(s32[256]{0:T(256)} %param.7) | copy-start | bytes 3076
  208.7 1.9 copy-start.3
  208.8 1.9 copy-start.2
  212.7 215.1 %all-reduce.3.cloned.1.call-start = ((), (), s32[]{:S(2)}) async-start(), calls=%async_computation.3 | async-start | bytes 294912
Sparse Core Ops, SparseCore 0:
  63.1 43.1 all-gather.1
  212.8 59.2 reduce-scatter.2
  275.5 152.2 all-reduce.2

commit v2 on v1

v2 whole, which is shorter than its diff:
```python
import jax
import jax.numpy as jnp
from jax import lax
from jax.sharding import PartitionSpec as P

softcap_value = 30.0
zloss_weight = 0.0001


def local(hidden, head, targets, probe_hidden, probe_head):
    voc_count = lax.axis_size("voc")
    vocab_width = head.shape[1]
    rows_here = hidden.shape[0]
    stacked = jnp.stack([hidden, probe_hidden])
    features = lax.all_gather(stacked, "voc", axis=2, tiled=True)
    gathered = lax.all_gather(features, "tok", axis=1, tiled=True)
    row_hidden = gathered[0]
    row_probe = gathered[1]
    logits = jnp.dot(row_hidden, head, preferred_element_type=jnp.float32)
    tangent = jnp.dot(row_probe, head, preferred_element_type=jnp.float32) + jnp.dot(
        row_hidden, probe_head, preferred_element_type=jnp.float32
    )
    capped = jnp.tanh(logits / softcap_value)
    cap_slope = 1.0 - capped * capped
    exponent = jnp.exp(softcap_value * capped)
    cap_tangent = cap_slope * tangent
    slope_tan = -2.0 / softcap_value * capped * cap_slope * tangent
    offset = (lax.axis_index("tok") * voc_count + lax.axis_index("voc")) * vocab_width
    columns = offset + lax.iota(jnp.int32, vocab_width)
    onehot = (targets[:, None] == columns[None, :]).astype(jnp.float32)

    weighted_slope = exponent * cap_slope
    weighted_tan = exponent * (cap_slope * cap_tangent + slope_tan)
    hi = lax.Precision.HIGHEST
    by_probe = lax.dot_general(
        jnp.stack([weighted_slope, onehot * cap_slope]), probe_head.astype(jnp.float32),
        (((2,), (1,)), ((), ())), precision=hi, preferred_element_type=jnp.float32,
    )
    by_head = lax.dot_general(
        jnp.stack([weighted_tan, weighted_slope, onehot * slope_tan]), head.astype(jnp.float32),
        (((2,), (1,)), ((), ())), precision=hi, preferred_element_type=jnp.float32,
    )
    partials = jnp.stack([by_probe[0] + by_head[0], by_head[1], by_probe[1] + by_head[2]])

    local_stats = jnp.stack([jnp.sum(exponent, axis=1), jnp.sum(exponent * cap_tangent, axis=1)])
    partials, local_stats = lax.optimization_barrier((partials, local_stats))
    summed = lax.psum_scatter(partials, "tok", scatter_dimension=1, tiled=True)
    reduced = lax.psum_scatter(summed, "voc", scatter_dimension=2, tiled=True)
    stats = lax.psum(local_stats, ("tok", "voc"))
    row_total = stats[0]
    probability = exponent / row_total[:, None]
    mean_tangent = stats[1] / row_total
    factor = 1.0 + 2.0 * zloss_weight * jnp.log(row_total)
    grad_cap = factor[:, None] * probability - onehot
    grad_tan = probability * (
        factor[:, None] * (cap_tangent - mean_tangent[:, None])
        + 2.0 * zloss_weight * mean_tangent[:, None]
    )
    dlogit = (grad_cap * cap_slope).astype(jnp.bfloat16)
    dlogit_tan = (grad_tan * cap_slope + grad_cap * slope_tan).astype(jnp.bfloat16)
    head_out = jnp.einsum(
        "krd,krv->dv", gathered, jnp.stack([dlogit_tan, dlogit]), preferred_element_type=jnp.float32
    )

    first_row = lax.axis_index("tok") * rows_here
    own_total = lax.dynamic_slice_in_dim(row_total, first_row, rows_here)
    own_mean = lax.dynamic_slice_in_dim(mean_tangent, first_row, rows_here)
    own_factor = lax.dynamic_slice_in_dim(factor, first_row, rows_here)
    scale_main = (own_factor / own_total)[:, None]
    scale_mean = ((2.0 * zloss_weight - own_factor) * own_mean / own_total)[:, None]
    hidden_out = scale_main * reduced[0] + scale_mean * reduced[1] - reduced[2]
    return (head_out, hidden_out)


def solution(mesh):
    return jax.shard_map(
        local,
        mesh=mesh,
        in_specs=(
            P("tok", "voc"),
            P(None, ("tok", "voc")),
            P(),
            P("tok", "voc"),
            P(None, ("tok", "voc")),
        ),
        out_specs=(P(None, ("tok", "voc")), P("tok", "voc")),
        check_vma=False,
    )
```

time: 436 us -> 391 us (0.90)
  the two profiles are of different devices: /device:TPU:2 before, /device:TPU:64 now
where the time goes in v2:
time: 391 us
  waiting for transfers between devices  196 us (50%)
  blocking collectives  149 us (38%)
  matrix products  15.4 us (4%)
  between operations  14.6 us (4%)
  other arithmetic  12.3 us (3%)
  local copies, waits for them, and re-layouts  4.4 us (1%)
    unnamed x4, waiting for transfers between devices  152 us
    psum x1, blocking collectives, local(): stats = lax.psum(local_stats, ('tok', 'voc'))  97.3 us
    all_gather x1, blocking collectives, local(): features = lax.all_gather(stacked, 'voc', axis=2, tiled=True)  51.2 us
    all_gather x1, waiting for transfers between devices, local(): gathered = lax.all_gather(features, 'tok', axis=1, tiled=True)  43.3 us
  transfers between devices with their start and end apart: 3, of which 2 were waited for; matrix products, arithmetic and copies ran while one was open for 2% of the time, Pallas kernels for 0%

profile of v2, /device:TPU:64, one launch (start us, length us, event | category | flops | bytes accessed | tf_op | source)
XLA Modules:
  0.0 390.9 jit_solution(4182991249321943812)
XLA Ops:
  7.2 0.0 all-gather.2.cloned.1.call-start
  7.2 0.9 pad_maximum_fusion.1
  8.1 0.7 copy.16
  8.8 51.2 %all_gather.6 = bf16[2,16,2304]{1,0,2:T(2,128)(2,1)S(1)} all-gather(bf16[2,16,72]{1,0,2:T(2,128)(2,1)} %copy.16), channel_id=1, replica_groups=mesh['tok'=16,'voc'=32] {'voc'}, dimensions={2}, use_global_device_ids=true | all-gather | bytes 152064 | tf_op jit(solution)/shard_map/all_gather | solution.py:15
  60.1 2.2 copy.17
  62.3 0.0 reduce-scatter.3.cloned.1.call-start
  62.4 43.3 %all-gather.2.cloned.1.call-done = bf16[2,256,2304]{2,1,0:T(8,128)(2,1)} async-done(((bf16[2,16,2304]{2,1,0:T(8,128)(2,1)}), bf16[2,256,2304]{2,1,0:T(8,128)(2,1)}) %all-gather.2.cloned.1.call-update) | async-done | bytes 2359312 | tf_op jit(solution)/shard_map/all_gather | solution.py:16
  105.7 2.0 fusion.7
  107.7 0.6 fusion.6
  108.3 0.6 fusion.5
  109.0 0.2 fusion.24
  109.1 4.1 %fusion.3 = f32[2,256,2304]{2,1,0:T(8,128)S(1)} fusion(bf16[2304,256]{1,0:T(8,128)(2,1)S(1)} %copy-done.4, f32[1,256,256]{1,2,0:T(8,128)S(1)} %get-tuple-element.17, f32[1,256,256]{1,2,0:T(8,128)S(1)} %get-tuple-element.18), kind=kOutput, calls=%fused_computation.9 | convolution fusion | flops 3624009728 | bytes 6422528 | tf_op jit(solution)/shard_map/dot_general | solution.py:35
  113.2 5.9 %fusion.1 = f32[3,256,2304]{2,1,0:T(8,128)S(1)} fusion(bf16[2304,256]{1,0:T(8,128)(2,1)S(1)} %copy-done, f32[1,256,256]{1,2,0:T(8,128)S(1)} %get-tuple-element.14, f32[1,256,256]{1,2,0:T(8,128)S(1)} %get-tuple-element.18, f32[1,256,256]{1,2,0:T(8,128)S(1)} %get-tuple-element.13), kind=kOutput, calls=%fused_computation.7 | convolution fusion | flops 5436211200 | bytes 9043968 | tf_op jit(solution)/shard_map/dot_general | solution.py:39
  119.2 2.3 slice_add_fusion.1
  121.5 5.1 %pad_maximum_fusion = f32[3,256,2304]{2,1,0:T(8,128)} fusion(f32[1,256,2304]{2,1,0:T(8,128)S(1)} %get-tuple-element.11, f32[1,256,2304]{2,1,0:T(8,128)} %get-tuple-element.12, f32[1,256,2304]{2,1,0:T(8,128)S(1)} %get-tuple-element.10), kind=kLoop, calls=%fused_computation | loop fusion | flops 3538944 | bytes 14155776 | tf_op jit(solution)/shard_map/stack | solution.py:43
  126.6 0.0 all-reduce.3.cloned.1.call-start
  126.7 1.4 dynamic-slice.1
  128.8 97.3 %psum.7 = f32[2,256]{1,0:T(2,128)S(1)} all-reduce(f32[2,256]{1,0:T(2,128)S(1)} %pad_maximum_fusion.2), channel_id=1, replica_groups=mesh['tok'=16,'voc'=32] {'tok','voc'}, use_global_device_ids=true, to_apply=%region_2.0 | all-reduce | flops 512 | bytes 4096 | tf_op jit(solution)/shard_map/psum | solution.py:49
  226.1 0.6 broadcast_multiply_fusion
  226.7 1.2 fusion.26
  227.9 0.6 bitcast_divide_fusion.1
  228.5 2.2 convolution_bitcast_fusion
  230.8 152.2 %all-reduce.3.cloned.1.call-done = f32[3,16,2304]{2,1,0:T(8,128)} async-done(((f32[3,16,2304]{2,1,0:T(8,128)}), f32[3,16,2304]{2,1,0:T(8,128)}) %all-reduce.3.cloned.1.call-update) | async-done | bytes 442384
  383.0 1.4 fusion.27
  (25 shorter events, 0.1 us)
Async XLA Ops:
  7.2 100.5 %copy-start = (bf16[2304,256]{1,0:T(8,128)(2,1)S(1)}, bf16[2304,256]{1,0:T(8,128)(2,1)}, u32[]{:S(2)}) copy-start(bf16[2304,256]{1,0:T(8,128)(2,1)} %param.6) | copy-start | bytes 3538948
  7.2 98.5 %copy-start.4 = (bf16[2304,256]{1,0:T(8,128)(2,1)S(1)}, bf16[2304,256]{1,0:T(8,128)(2,1)}, u32[]{:S(2)}) copy-start(bf16[2304,256]{1,0:T(8,128)(2,1)} %param.9) | copy-start | bytes 3538948
  7.2 98.5 %all-gather.2.cloned.1.call-start = ((), (), s32[]{:S(2)}) async-start(), calls=%async_computation.1 | async-start | bytes 2506752 | tf_op jit(solution)/shard_map/all_gather | solution.py:16
  62.3 164.4 %reduce-scatter.3.cloned.1.call-start = ((), (), s32[]{:S(2)}) async-start(), calls=%async_computation.2 | async-start | bytes 7520256 | tf_op jit(solution)/shard_map/reduce_scatter | solution.py:47
  62.4 46.6 %copy-start.7 = (s32[256]{0:T(256)}, s32[256]{0:T(256)S(1)}, u32[]{:S(2)}) copy-start(s32[256]{0:T(256)S(1)} %iota_add_fusion) | copy-start | bytes 3076
  105.7 2.0 copy-start.1
  107.7 1.2 copy-start.6
  108.3 4.9 %copy-start.5 = (f32[256,256]{0,1:T(8,128)}, f32[256,256]{0,1:T(8,128)S(1)}, u32[]{:S(2)}) copy-start(f32[256,256]{0,1:T(8,128)S(1)} %fusion.6) | copy-start | bytes 786436
  109.0 4.3 %copy-start.3 = (f32[256,256]{0,1:T(8,128)}, f32[256,256]{0,1:T(8,128)S(1)}, u32[]{:S(2)}) copy-start(f32[256,256]{0,1:T(8,128)S(1)} %fusion.5) | copy-start | bytes 786436
  126.6 101.9 %copy-start.2 = (bf16[2,256,2304]{2,1,0:T(8,128)(2,1)S(1)}, bf16[2,256,2304]{2,1,0:T(8,128)(2,1)}, u32[]{:S(2)}) copy-start(bf16[2,256,2304]{2,1,0:T(8,128)(2,1)} %all-gather.2.cloned.1.call-done) | copy-start | bytes 7077892
  126.6 256.3 %all-reduce.3.cloned.1.call-start = ((), (), s32[]{:S(2)}) async-start(), calls=%async_computation.3 | async-start | bytes 884736
  228.5 154.4 %copy-start.8 = (f32[16]{0:T(128)S(1)}, f32[16]{0:T(128)}, u32[]{:S(2)}) copy-start(f32[16]{0:T(128)} %get-tuple-element.20) | copy-start | bytes 196
Sparse Core Ops, SparseCore 0:
  62.4 43.2 all-gather.1
  126.8 67.1 reduce-scatter.2
  226.8 156.1 all-reduce.2

commit v3 on v2

--- a/solution.py
+++ b/solution.py
@@ -1,18 +1,19 @@
 import jax
 import jax.numpy as jnp
 from jax import lax
-from jax.sharding import PartitionSpec as P
+import numpy as np
+from jax.sharding import Mesh, PartitionSpec as P
 
 softcap_value = 30.0
 zloss_weight = 0.0001
 
 
 def local(hidden, head, targets, probe_hidden, probe_head):
-    voc_count = lax.axis_size("voc")
+    voc_count = lax.axis_size("vy") * lax.axis_size("vx")
     vocab_width = head.shape[1]
     rows_here = hidden.shape[0]
     stacked = jnp.stack([hidden, probe_hidden])
-    features = lax.all_gather(stacked, "voc", axis=2, tiled=True)
+    features = lax.all_gather(lax.all_gather(stacked, "vx", axis=2, tiled=True), "vy", axis=2, tiled=True)
     gathered = lax.all_gather(features, "tok", axis=1, tiled=True)
     row_hidden = gathered[0]
     row_probe = gathered[1]
@@ -25,7 +26,8 @@
     exponent = jnp.exp(softcap_value * capped)
     cap_tangent = cap_slope * tangent
     slope_tan = -2.0 / softcap_value * capped * cap_slope * tangent
-    offset = (lax.axis_index("tok") * voc_count + lax.axis_index("voc")) * vocab_width
+    voc_index = lax.axis_index("vy") * lax.axis_size("vx") + lax.axis_index("vx")
+    offset = (lax.axis_index("tok") * voc_count + voc_index) * vocab_width
     columns = offset + lax.iota(jnp.int32, vocab_width)
     onehot = (targets[:, None] == columns[None, :]).astype(jnp.float32)
 
@@ -45,8 +47,10 @@
     local_stats = jnp.stack([jnp.sum(exponent, axis=1), jnp.sum(exponent * cap_tangent, axis=1)])
     partials, local_stats = lax.optimization_barrier((partials, local_stats))
     summed = lax.psum_scatter(partials, "tok", scatter_dimension=1, tiled=True)
-    reduced = lax.psum_scatter(summed, "voc", scatter_dimension=2, tiled=True)
-    stats = lax.psum(local_stats, ("tok", "voc"))
+    stats = lax.psum(lax.psum(lax.psum(local_stats, "tok"), "vy"), "vx")
+    kinds, rows, width = summed.shape
+    blocks = summed.reshape(kinds, rows, voc_count, width // voc_count).transpose(2, 0, 1, 3)
+    reduced = jnp.sum(lax.all_to_all(blocks, ("vy", "vx"), 0, 0, tiled=True), axis=0)
     row_total = stats[0]
     probability = exponent / row_total[:, None]
     mean_tangent = stats[1] / row_total
@@ -73,16 +77,20 @@
 
 
 def solution(mesh):
+    tok_size, voc_size = mesh.devices.shape
+    x_size = 4 if voc_size % 4 == 0 else 1
+    split = Mesh(np.asarray(mesh.devices).reshape(tok_size, voc_size // x_size, x_size), ("tok", "vy", "vx"))
+    voc = ("vy", "vx")
     return jax.shard_map(
         local,
-        mesh=mesh,
+        mesh=split,
         in_specs=(
-            P("tok", "voc"),
-            P(None, ("tok", "voc")),
+            P("tok", voc),
+            P(None, ("tok",) + voc),
             P(),
-            P("tok", "voc"),
-            P(None, ("tok", "voc")),
+            P("tok", voc),
+            P(None, ("tok",) + voc),
         ),
-        out_specs=(P(None, ("tok", "voc")), P("tok", "voc")),
+        out_specs=(P(None, ("tok",) + voc), P("tok", voc)),
         check_vma=False,
     )

time: 391 us -> 232 us (0.59)
  the two profiles are of different devices: /device:TPU:64 before, /device:TPU:2 now
where the time goes in v3:
time: 232 us
  blocking collectives  92.5 us (40%)
  waiting for transfers between devices  79.9 us (34%)
  matrix products  15.4 us (7%)
  between operations  14.2 us (6%)
  other arithmetic  12.1 us (5%)
  starting transfers between devices  9.91 us (4%)
  local copies, waits for them, and re-layouts  7.57 us (3%)
    psum x3, blocking collectives, local(): stats = lax.psum(lax.psum(lax.psum(local_stats, 'tok'), 'vy'), 'vx')  50.6 us
    all_gather x1, waiting for transfers between devices, local(): gathered = lax.all_gather(features, 'tok', axis=1, tiled=True)  45 us
    all_gather x1, blocking collectives, local(): lax.all_gather(lax.all_gather(stacked, 'vx', axis=2, tiled=True), 'vy', a...  27.3 us
    reduce_scatter x1, waiting for transfers between devices, local(): summed = lax.psum_scatter(partials, 'tok', scatter_dimension=1, tiled=True)  19.5 us
    all_to_all x1, waiting for transfers between devices, local(): lax.all_to_all(blocks, ('vy', 'vx'), 0, 0, tiled=True)  15.3 us
    all_gather x1, blocking collectives, local(): lax.all_gather(stacked, 'vx', axis=2, tiled=True)  14.7 us
    all_to_all x1, starting transfers between devices, local(): lax.all_to_all(blocks, ('vy', 'vx'), 0, 0, tiled=True)  9.83 us
    dot_general x1, matrix products, local(): lax.dot_general(jnp.stack([weighted_tan, weighted_slope, onehot * slope_t...  5.92 us
  transfers between devices with their start and end apart: 3, of which 3 were waited for; matrix products, arithmetic and copies ran while one was open for 2% of the time, Pallas kernels for 0%

profile of v3, /device:TPU:2, one launch (start us, length us, event | category | flops | bytes accessed | tf_op | source)
XLA Modules:
  0.0 231.6 jit_solution(1896644353649314430)
XLA Ops:
  7.2 0.8 pad_maximum_fusion.1
  8.1 14.7 %all_gather.9 = bf16[2,16,288]{1,0,2:T(2,128)(2,1)S(1)} all-gather(bf16[2,16,72]{1,0,2:T(2,128)(2,1)S(1)} %copy.17), channel_id=1, replica_groups=mesh['tok'=16,'vy'=8,'vx'=4] {'vx'}, dimensions={2}, use_global_device_ids=true | all-gather | bytes 23040 | tf_op jit(solution)/shard_map/all_gather | solution.py:16
  22.8 27.3 %all_gather.10 = bf16[2,16,2304]{1,0,2:T(2,128)(2,1)S(1)} all-gather(bf16[2,16,288]{1,0,2:T(2,128)(2,1)S(1)} %all_gather.9), channel_id=1, replica_groups=mesh['tok'=16,'vy'=8,'vx'=4] {'vy'}, dimensions={2}, use_global_device_ids=true | all-gather | bytes 165888 | tf_op jit(solution)/shard_map/all_gather | solution.py:16
  50.1 2.2 copy.18
  52.4 45.0 %all-gather.2.cloned.1.call-done = bf16[2,256,2304]{2,1,0:T(8,128)(2,1)} async-done(((bf16[2,16,2304]{2,1,0:T(8,128)(2,1)}), bf16[2,256,2304]{2,1,0:T(8,128)(2,1)}) %all-gather.2.cloned.1.call-update) | async-done | bytes 2359312 | tf_op jit(solution)/shard_map/all_gather | solution.py:17
  97.4 2.0 fusion.6
  99.4 0.6 fusion.7
  100.0 0.6 fusion.5
  100.8 4.1 %fusion.3 = f32[2,256,2304]{2,1,0:T(8,128)S(1)} fusion(bf16[2304,256]{1,0:T(8,128)(2,1)S(1)} %copy-done.4, f32[1,256,256]{1,2,0:T(8,128)S(1)} %get-tuple-element.17, f32[1,256,256]{1,2,0:T(8,128)S(1)} %get-tuple-element.18), kind=kOutput, calls=%fused_computation.9 | convolution fusion | flops 3624009728 | bytes 6422528 | tf_op jit(solution)/shard_map/dot_general | solution.py:37
  104.9 5.9 %fusion.1 = f32[3,256,2304]{2,1,0:T(8,128)S(1)} fusion(bf16[2304,256]{1,0:T(8,128)(2,1)S(1)} %copy-done, f32[1,256,256]{1,2,0:T(8,128)S(1)} %get-tuple-element.14, f32[1,256,256]{1,2,0:T(8,128)S(1)} %get-tuple-element.18, f32[1,256,256]{1,2,0:T(8,128)S(1)} %get-tuple-element.13), kind=kOutput, calls=%fused_computation.7 | convolution fusion | flops 5436211200 | bytes 9043968 | tf_op jit(solution)/shard_map/dot_general | solution.py:41
  110.9 2.3 slice_add_fusion.1
  113.1 5.1 %pad_maximum_fusion = f32[3,256,2304]{2,1,0:T(8,128)} fusion(f32[1,256,2304]{2,1,0:T(8,128)S(1)} %get-tuple-element.11, f32[1,256,2304]{2,1,0:T(8,128)} %get-tuple-element.12, f32[1,256,2304]{2,1,0:T(8,128)S(1)} %get-tuple-element.10), kind=kLoop, calls=%fused_computation | loop fusion | flops 3538944 | bytes 14155776 | tf_op jit(solution)/shard_map/stack | solution.py:45
  118.3 25.0 %psum.21 = f32[2,256]{1,0:T(2,128)S(1)} all-reduce(f32[2,256]{1,0:T(2,128)S(1)} %pad_maximum_fusion.2), channel_id=1, replica_groups=mesh['tok'=16,'vy'=8,'vx'=4] {'tok'}, use_global_device_ids=true, to_apply=%region_2.0 | all-reduce | flops 512 | bytes 4096 | tf_op jit(solution)/shard_map/psum | solution.py:50
  143.4 17.0 %psum.22 = f32[2,256]{1,0:T(2,128)S(1)} all-reduce(f32[2,256]{1,0:T(2,128)S(1)} %psum.21), channel_id=1, replica_groups=mesh['tok'=16,'vy'=8,'vx'=4] {'vy'}, use_global_device_ids=true, to_apply=%region_3.0 | all-reduce | flops 512 | bytes 4096 | tf_op jit(solution)/shard_map/psum | solution.py:50
  160.3 8.6 %psum.23 = f32[2,256]{1,0:T(2,128)S(1)} all-reduce(f32[2,256]{1,0:T(2,128)S(1)} %psum.22), channel_id=1, replica_groups=mesh['tok'=16,'vy'=8,'vx'=4] {'vx'}, use_global_device_ids=true, to_apply=%region_4.0 | all-reduce | flops 512 | bytes 4096 | tf_op jit(solution)/shard_map/psum | solution.py:50
  168.9 19.5 %reduce-scatter.2.cloned.1.call-done = f32[3,16,2304]{2,1,0:T(8,128)} async-done(((f32[3,256,2304]{2,1,0:T(8,128)}), f32[3,16,2304]{2,1,0:T(8,128)}) %reduce-scatter.2.cloned.1.call-update) | async-done | bytes 442384 | tf_op jit(solution)/shard_map/reduce_scatter | solution.py:49
  188.4 2.7 %reshape.40 = f32[3,16,32,72]{3,2,1,0:T(8,128)} reshape(f32[3,16,2304]{2,1,0:T(8,128)} %reduce-scatter.2.cloned.1.call-done) | data formatting | bytes 884736 | tf_op jit(solution)/shard_map/reshape | solution.py:52
  191.1 2.5 %copy.27 = f32[3,16,32,72]{3,1,0,2:T(8,128)} copy(f32[3,16,32,72]{3,2,1,0:T(8,128)} %reshape.40) | data formatting | bytes 884736 | tf_op jit(solution)/shard_map/reshape | solution.py:52
  193.6 9.8 %all-to-all-start = ((f32[32,3,16,72]{3,2,1,0:T(8,128)}), f32[32,3,16,72]{3,2,1,0:T(8,128)}, u32[]{:S(2)}, u32[]{:S(2)}) async-start(f32[32,3,16,72]{3,2,1,0:T(8,128)} %bitcast.63), calls=%async_computation.1 | async-start | bytes 1572864 | tf_op jit(solution)/shard_map/all_to_all | solution.py:53
  204.1 1.2 fusion.26
  205.3 2.2 convolution_bitcast_fusion
  207.6 15.3 %all-to-all-done = f32[32,3,16,72]{3,2,1,0:T(8,128)} async-done(((f32[32,3,16,72]{3,2,1,0:T(8,128)}), f32[32,3,16,72]{3,2,1,0:T(8,128)}, u32[]{:S(2)}, u32[]{:S(2)}) %all-to-all-start) | async-done | bytes 442400 | tf_op jit(solution)/shard_map/all_to_all | solution.py:53
  222.9 1.2 reduce_sum.29
  224.1 0.7 fusion.27
  (27 shorter events, 1.1 us)
Async XLA Ops:
  7.2 90.2 %copy-start = (bf16[2304,256]{1,0:T(8,128)(2,1)S(1)}, bf16[2304,256]{1,0:T(8,128)(2,1)}, u32[]{:S(2)}) copy-start(bf16[2304,256]{1,0:T(8,128)(2,1)} %param.6) | copy-start | bytes 3538948
  7.2 90.2 %all-gather.2.cloned.1.call-start = ((), (), s32[]{:S(2)}) async-start(), calls=%async_computation.2 | async-start | bytes 2506752 | tf_op jit(solution)/shard_map/all_gather | solution.py:17
  50.1 49.3 %copy-start.4 = (bf16[2304,256]{1,0:T(8,128)(2,1)S(1)}, bf16[2304,256]{1,0:T(8,128)(2,1)}, u32[]{:S(2)}) copy-start(bf16[2304,256]{1,0:T(8,128)(2,1)} %param.9) | copy-start | bytes 3538948
  52.3 136.1 %reduce-scatter.2.cloned.1.call-start = ((), (), s32[]{:S(2)}) async-start(), calls=%async_computation.3 | async-start | bytes 7520256 | tf_op jit(solution)/shard_map/reduce_scatter | solution.py:49
  97.4 2.0 copy-start.1
  99.4 1.2 copy-start.5
  99.4 1.2 copy-start.6
  100.6 4.3 %copy-start.3 = (f32[256,256]{0,1:T(8,128)}, f32[256,256]{0,1:T(8,128)S(1)}, u32[]{:S(2)}) copy-start(f32[256,256]{0,1:T(8,128)S(1)} %fusion.5) | copy-start | bytes 786436
  168.9 36.4 %copy-start.2 = (bf16[2,256,2304]{2,1,0:T(8,128)(2,1)S(1)}, bf16[2,256,2304]{2,1,0:T(8,128)(2,1)}, u32[]{:S(2)}) copy-start(bf16[2,256,2304]{2,1,0:T(8,128)(2,1)} %all-gather.2.cloned.1.call-done) | copy-start | bytes 7077892
  193.6 29.3 %all-to-all-start = ((f32[32,3,16,72]{3,2,1,0:T(8,128)}), f32[32,3,16,72]{3,2,1,0:T(8,128)}, u32[]{:S(2)}, u32[]{:S(2)}) async-start(f32[32,3,16,72]{3,2,1,0:T(8,128)} %bitcast.63), calls=%async_computation.1 | async-start | bytes 1572864 | tf_op jit(solution)/shard_map/all_to_all | solution.py:53
  205.3 18.8 %copy-start.7 = (f32[16]{0:T(128)S(1)}, f32[16]{0:T(128)}, u32[]{:S(2)}) copy-start(f32[16]{0:T(128)} %get-tuple-element.20) | copy-start | bytes 196
Sparse Core Ops, SparseCore 0:
  52.4 44.8 all-gather.1
  118.4 69.9 reduce-scatter.1

commit v4 on v3

--- a/solution.py
+++ b/solution.py
@@ -13,7 +13,9 @@
     vocab_width = head.shape[1]
     rows_here = hidden.shape[0]
     stacked = jnp.stack([hidden, probe_hidden])
-    features = lax.all_gather(lax.all_gather(stacked, "vx", axis=2, tiled=True), "vy", axis=2, tiled=True)
+    copies = jnp.broadcast_to(stacked[None], (voc_count,) + stacked.shape)
+    blocks = lax.all_to_all(copies, ("vy", "vx"), 0, 0, tiled=True)
+    features = blocks.transpose(1, 2, 0, 3).reshape(2, rows_here, voc_count * stacked.shape[2])
     gathered = lax.all_gather(features, "tok", axis=1, tiled=True)
     row_hidden = gathered[0]
     row_probe = gathered[1]

time: 232 us -> 209 us (0.901)
  blocking collectives: 92.5 us -> 72 us
    all_gather x2 -> x0, blocking collectives: 42 us -> none  [the longest x1 27.3 us: local(): lax.all_gather(lax.all_gather(stacked, 'vx', axis=2, tiled=True), 'vy', a...]
    all_to_all x0 -> x1, blocking collectives: none -> 21.4 us  [local(): blocks = lax.all_to_all(copies, ('vy', 'vx'), 0, 0, tiled=True)]
where the time goes in v4:
time: 209 us; the launch traced here: 208 us
  waiting for transfers between devices  78.1 us (37%)
  blocking collectives  72 us (34%)
  matrix products  15.4 us (7%)
  between operations  14.2 us (7%)
  other arithmetic  12.1 us (6%)
  starting transfers between devices  9.91 us (5%)
  local copies, waits for them, and re-layouts  6.41 us (3%)
    psum x3, blocking collectives, local(): stats = lax.psum(lax.psum(lax.psum(local_stats, 'tok'), 'vy'), 'vx')  50.6 us
    all_gather x1, waiting for transfers between devices, local(): gathered = lax.all_gather(features, 'tok', axis=1, tiled=True)  43.2 us
    all_to_all x1, blocking collectives, local(): blocks = lax.all_to_all(copies, ('vy', 'vx'), 0, 0, tiled=True)  21.4 us
    reduce_scatter x1, waiting for transfers between devices, local(): summed = lax.psum_scatter(partials, 'tok', scatter_dimension=1, tiled=True)  19.5 us
    all_to_all x1, waiting for transfers between devices, local(): lax.all_to_all(blocks, ('vy', 'vx'), 0, 0, tiled=True)  15.3 us
    all_to_all x1, starting transfers between devices, local(): lax.all_to_all(blocks, ('vy', 'vx'), 0, 0, tiled=True)  9.83 us
    dot_general x1, matrix products, local(): lax.dot_general(jnp.stack([weighted_tan, weighted_slope, onehot * slope_t...  5.92 us
    reshape x2, local copies, waits for them, and re-layouts, local(): summed.reshape(kinds, rows, voc_count, width // voc_count)  5.19 us
  transfers between devices with their start and end apart: 3, of which 3 were waited for; matrix products, arithmetic and copies ran while one was open for 2% of the time, Pallas kernels for 0%

profile of v4, /device:TPU:2, one launch (start us, length us, event | category | flops | bytes accessed | tf_op | source)
XLA Modules:
  0.0 208.2 jit_solution(698831221928783216)
XLA Ops:
  7.2 0.8 pad_maximum_fusion.1
  8.1 21.4 %all_to_all.10 = bf16[32,2,16,72]{3,2,1,0:T(8,128)(2,1)S(1)} all-to-all(bf16[32,2,16,72]{3,2,1,0:T(8,128)(2,1)S(1)} %broadcast_in_dim.2), channel_id=1, replica_groups=mesh['tok'=16,'vy'=8,'vx'=4] {'vy','vx'}, dimensions={0} | all-to-all | bytes 294912 | tf_op jit(solution)/shard_map/all_to_all | solution.py:17
  29.6 1.0 reshape.44
  30.7 43.2 %all-gather.2.cloned.1.call-done = bf16[2,256,2304]{2,1,0:T(8,128)(2,1)} async-done(((bf16[2,16,2304]{2,1,0:T(8,128)(2,1)}), bf16[2,256,2304]{2,1,0:T(8,128)(2,1)}) %all-gather.2.cloned.1.call-update) | async-done | bytes 2359312 | tf_op jit(solution)/shard_map/all_gather | solution.py:19
  73.9 2.0 fusion.6
  75.9 0.6 fusion.7
  76.5 0.6 fusion.5
  77.4 4.1 %fusion.3 = f32[2,256,2304]{2,1,0:T(8,128)S(1)} fusion(bf16[2304,256]{1,0:T(8,128)(2,1)S(1)} %copy-done.4, f32[1,256,256]{1,2,0:T(8,128)S(1)} %get-tuple-element.17, f32[1,256,256]{1,2,0:T(8,128)S(1)} %get-tuple-element.18), kind=kOutput, calls=%fused_computation.9 | convolution fusion | flops 3624009728 | bytes 6422528 | tf_op jit(solution)/shard_map/dot_general | solution.py:39
  81.5 5.9 %fusion.1 = f32[3,256,2304]{2,1,0:T(8,128)S(1)} fusion(bf16[2304,256]{1,0:T(8,128)(2,1)S(1)} %copy-done, f32[1,256,256]{1,2,0:T(8,128)S(1)} %get-tuple-element.14, f32[1,256,256]{1,2,0:T(8,128)S(1)} %get-tuple-element.18, f32[1,256,256]{1,2,0:T(8,128)S(1)} %get-tuple-element.13), kind=kOutput, calls=%fused_computation.7 | convolution fusion | flops 5436211200 | bytes 9043968 | tf_op jit(solution)/shard_map/dot_general | solution.py:43
  87.4 2.3 %slice_add_fusion.1 = (f32[1,256,2304]{2,1,0:T(8,128)S(1)}, f32[1,256,2304]{2,1,0:T(8,128)S(1)}, f32[1,256,2304]{2,1,0:T(8,128)}) fusion(f32[3,256,2304]{2,1,0:T(8,128)S(1)} %fusion.1, f32[2,256,2304]{2,1,0:T(8,128)S(1)} %fusion.3), kind=kLoop, calls=%fused_computation.3 | loop fusion | flops 1179648 | bytes 18874368 | tf_op jit(solution)/shard_map/add | solution.py:47
  89.7 5.1 %pad_maximum_fusion = f32[3,256,2304]{2,1,0:T(8,128)} fusion(f32[1,256,2304]{2,1,0:T(8,128)S(1)} %get-tuple-element.11, f32[1,256,2304]{2,1,0:T(8,128)} %get-tuple-element.12, f32[1,256,2304]{2,1,0:T(8,128)S(1)} %get-tuple-element.10), kind=kLoop, calls=%fused_computation | loop fusion | flops 3538944 | bytes 14155776 | tf_op jit(solution)/shard_map/stack | solution.py:47
  94.8 25.1 %psum.21 = f32[2,256]{1,0:T(2,128)S(1)} all-reduce(f32[2,256]{1,0:T(2,128)S(1)} %pad_maximum_fusion.2), channel_id=1, replica_groups=mesh['tok'=16,'vy'=8,'vx'=4] {'tok'}, use_global_device_ids=true, to_apply=%region_2.0 | all-reduce | flops 512 | bytes 4096 | tf_op jit(solution)/shard_map/psum | solution.py:52
  120.0 16.9 %psum.22 = f32[2,256]{1,0:T(2,128)S(1)} all-reduce(f32[2,256]{1,0:T(2,128)S(1)} %psum.21), channel_id=1, replica_groups=mesh['tok'=16,'vy'=8,'vx'=4] {'vy'}, use_global_device_ids=true, to_apply=%region_3.0 | all-reduce | flops 512 | bytes 4096 | tf_op jit(solution)/shard_map/psum | solution.py:52
  136.8 8.6 %psum.23 = f32[2,256]{1,0:T(2,128)S(1)} all-reduce(f32[2,256]{1,0:T(2,128)S(1)} %psum.22), channel_id=1, replica_groups=mesh['tok'=16,'vy'=8,'vx'=4] {'vx'}, use_global_device_ids=true, to_apply=%region_4.0 | all-reduce | flops 512 | bytes 4096 | tf_op jit(solution)/shard_map/psum | solution.py:52
  145.4 19.5 %reduce-scatter.2.cloned.1.call-done = f32[3,16,2304]{2,1,0:T(8,128)} async-done(((f32[3,256,2304]{2,1,0:T(8,128)}), f32[3,16,2304]{2,1,0:T(8,128)}) %reduce-scatter.2.cloned.1.call-update) | async-done | bytes 442384 | tf_op jit(solution)/shard_map/reduce_scatter | solution.py:51
  165.0 2.7 %reshape.45 = f32[3,16,32,72]{3,2,1,0:T(8,128)} reshape(f32[3,16,2304]{2,1,0:T(8,128)} %reduce-scatter.2.cloned.1.call-done) | data formatting | bytes 884736 | tf_op jit(solution)/shard_map/reshape | solution.py:54
  167.7 2.5 %copy.19 = f32[3,16,32,72]{3,1,0,2:T(8,128)} copy(f32[3,16,32,72]{3,2,1,0:T(8,128)} %reshape.45) | data formatting | bytes 884736 | tf_op jit(solution)/shard_map/reshape | solution.py:54
  170.1 9.8 %all-to-all-start.1 = ((f32[32,3,16,72]{3,2,1,0:T(8,128)}), f32[32,3,16,72]{3,2,1,0:T(8,128)}, u32[]{:S(2)}, u32[]{:S(2)}) async-start(f32[32,3,16,72]{3,2,1,0:T(8,128)} %bitcast.66), calls=%async_computation.2 | async-start | bytes 1572864 | tf_op jit(solution)/shard_map/all_to_all | solution.py:55
  180.0 0.6 bitcast_divide_fusion.1
  180.6 1.2 fusion.26
  181.9 2.2 %convolution_bitcast_fusion = f32[2304,256]{1,0:T(8,128)} fusion(bf16[2,256,2304]{2,1,0:T(8,128)(2,1)S(1)} %copy-done.2, bf16[1,256,256]{1,2,0:T(8,128)(2,1)S(1)} %get-tuple-element.16, bf16[1,256,256]{1,2,0:T(8,128)(2,1)S(1)} %get-tuple-element.15), kind=kOutput, calls=%fused_computation.1 | convolution fusion | flops 604110848 | bytes 4980736 | tf_op jit(solution)/shard_map/krd,krv->dv/dot_general | solution.py:67
  184.1 15.3 %all-to-all-done.1 = f32[32,3,16,72]{3,2,1,0:T(8,128)} async-done(((f32[32,3,16,72]{3,2,1,0:T(8,128)}), f32[32,3,16,72]{3,2,1,0:T(8,128)}, u32[]{:S(2)}, u32[]{:S(2)}) %all-to-all-start.1) | async-done | bytes 442400 | tf_op jit(solution)/shard_map/all_to_all | solution.py:55
  199.4 1.2 reduce_sum.29
  200.6 0.7 fusion.27
  (27 shorter events, 0.5 us)
Async XLA Ops:
  7.2 66.7 %copy-start = (bf16[2304,256]{1,0:T(8,128)(2,1)S(1)}, bf16[2304,256]{1,0:T(8,128)(2,1)}, u32[]{:S(2)}) copy-start(bf16[2304,256]{1,0:T(8,128)(2,1)} %param.6) | copy-start | bytes 3538948
  7.2 66.7 %all-gather.2.cloned.1.call-start = ((), (), s32[]{:S(2)}) async-start(), calls=%async_computation.3 | async-start | bytes 2506752 | tf_op jit(solution)/shard_map/all_gather | solution.py:19
  8.0 67.9 %copy-start.4 = (bf16[2304,256]{1,0:T(8,128)(2,1)S(1)}, bf16[2304,256]{1,0:T(8,128)(2,1)}, u32[]{:S(2)}) copy-start(bf16[2304,256]{1,0:T(8,128)(2,1)} %param.9) | copy-start | bytes 3538948
  30.6 134.3 %reduce-scatter.2.cloned.1.call-start = ((), (), s32[]{:S(2)}) async-start(), calls=%async_computation.4 | async-start | bytes 7520256 | tf_op jit(solution)/shard_map/reduce_scatter | solution.py:51
  73.9 2.0 copy-start.1
  75.9 1.2 copy-start.5
  75.9 1.2 copy-start.6
  77.2 4.3 %copy-start.3 = (f32[256,256]{0,1:T(8,128)}, f32[256,256]{0,1:T(8,128)S(1)}, u32[]{:S(2)}) copy-start(f32[256,256]{0,1:T(8,128)S(1)} %fusion.5) | copy-start | bytes 786436
  145.4 36.4 %copy-start.2 = (bf16[2,256,2304]{2,1,0:T(8,128)(2,1)S(1)}, bf16[2,256,2304]{2,1,0:T(8,128)(2,1)}, u32[]{:S(2)}) copy-start(bf16[2,256,2304]{2,1,0:T(8,128)(2,1)} %all-gather.2.cloned.1.call-done) | copy-start | bytes 7077892
  170.1 29.3 %all-to-all-start.1 = ((f32[32,3,16,72]{3,2,1,0:T(8,128)}), f32[32,3,16,72]{3,2,1,0:T(8,128)}, u32[]{:S(2)}, u32[]{:S(2)}) async-start(f32[32,3,16,72]{3,2,1,0:T(8,128)} %bitcast.66), calls=%async_computation.2 | async-start | bytes 1572864 | tf_op jit(solution)/shard_map/all_to_all | solution.py:55
  181.9 18.8 %copy-start.7 = (f32[16]{0:T(128)S(1)}, f32[16]{0:T(128)}, u32[]{:S(2)}) copy-start(f32[16]{0:T(128)} %get-tuple-element.20) | copy-start | bytes 196
Sparse Core Ops, SparseCore 0:
  30.7 43.1 all-gather.1
  95.0 69.9 reduce-scatter.1

commit v5 on v4

--- a/solution.py
+++ b/solution.py
@@ -16,7 +16,7 @@
     copies = jnp.broadcast_to(stacked[None], (voc_count,) + stacked.shape)
     blocks = lax.all_to_all(copies, ("vy", "vx"), 0, 0, tiled=True)
     features = blocks.transpose(1, 2, 0, 3).reshape(2, rows_here, voc_count * stacked.shape[2])
-    gathered = lax.all_gather(features, "tok", axis=1, tiled=True)
+    gathered = lax.all_gather(features, ("tz", "tc"), axis=1, tiled=True)
     row_hidden = gathered[0]
     row_probe = gathered[1]
     logits = jnp.dot(row_hidden, head, preferred_element_type=jnp.float32)
@@ -29,7 +29,7 @@
     cap_tangent = cap_slope * tangent
     slope_tan = -2.0 / softcap_value * capped * cap_slope * tangent
     voc_index = lax.axis_index("vy") * lax.axis_size("vx") + lax.axis_index("vx")
-    offset = (lax.axis_index("tok") * voc_count + voc_index) * vocab_width
+    offset = ((lax.axis_index("tz") * lax.axis_size("tc") + lax.axis_index("tc")) * voc_count + voc_index) * vocab_width
     columns = offset + lax.iota(jnp.int32, vocab_width)
     onehot = (targets[:, None] == columns[None, :]).astype(jnp.float32)
 
@@ -48,8 +48,8 @@
 
     local_stats = jnp.stack([jnp.sum(exponent, axis=1), jnp.sum(exponent * cap_tangent, axis=1)])
     partials, local_stats = lax.optimization_barrier((partials, local_stats))
-    summed = lax.psum_scatter(partials, "tok", scatter_dimension=1, tiled=True)
-    stats = lax.psum(lax.psum(lax.psum(local_stats, "tok"), "vy"), "vx")
+    summed = lax.psum_scatter(partials, ("tz", "tc"), scatter_dimension=1, tiled=True)
+    stats = lax.psum(lax.psum(lax.psum(lax.psum(local_stats, "tc"), "tz"), "vy"), "vx")
     kinds, rows, width = summed.shape
     blocks = summed.reshape(kinds, rows, voc_count, width // voc_count).transpose(2, 0, 1, 3)
     reduced = jnp.sum(lax.all_to_all(blocks, ("vy", "vx"), 0, 0, tiled=True), axis=0)
@@ -68,7 +68,7 @@
         "krd,krv->dv", gathered, jnp.stack([dlogit_tan, dlogit]), preferred_element_type=jnp.float32
     )
 
-    first_row = lax.axis_index("tok") * rows_here
+    first_row = (lax.axis_index("tz") * lax.axis_size("tc") + lax.axis_index("tc")) * rows_here
     own_total = lax.dynamic_slice_in_dim(row_total, first_row, rows_here)
     own_mean = lax.dynamic_slice_in_dim(mean_tangent, first_row, rows_here)
     own_factor = lax.dynamic_slice_in_dim(factor, first_row, rows_here)
@@ -80,19 +80,24 @@
 
 def solution(mesh):
     tok_size, voc_size = mesh.devices.shape
+    c_size = 2 if tok_size % 2 == 0 else 1
     x_size = 4 if voc_size % 4 == 0 else 1
-    split = Mesh(np.asarray(mesh.devices).reshape(tok_size, voc_size // x_size, x_size), ("tok", "vy", "vx"))
+    split = Mesh(
+        np.asarray(mesh.devices).reshape(tok_size // c_size, c_size, voc_size // x_size, x_size),
+        ("tz", "tc", "vy", "vx"),
+    )
+    tok = ("tz", "tc")
     voc = ("vy", "vx")
     return jax.shard_map(
         local,
         mesh=split,
         in_specs=(
-            P("tok", voc),
-            P(None, ("tok",) + voc),
+            P(tok, voc),
+            P(None, tok + voc),
             P(),
-            P("tok", voc),
-            P(None, ("tok",) + voc),
+            P(tok, voc),
+            P(None, tok + voc),
         ),
-        out_specs=(P(None, ("tok",) + voc), P("tok", voc)),
+        out_specs=(P(None, tok + voc), P(tok, voc)),
         check_vma=False,
     )

time: 209 us -> 209 us (level)
  blocking collectives: 72 us -> 65.1 us
  waiting for transfers between devices: 78.1 us -> 84.9 us
    psum x3 -> x4, blocking collectives: 50.6 us -> 43.7 us  [the longest x1 17 us: local(): lax.psum(lax.psum(lax.psum(local_stats, 'tc'), 'tz'), 'vy')]
    reduce_scatter x1, waiting for transfers between devices: 19.5 us -> 26.2 us  [local(): lax.psum_scatter(partials, ('tz', 'tc'), scatter_dimension=1, tiled=True)]
where the time goes in v5:
time: 209 us; the launch traced here: 208 us
  waiting for transfers between devices  84.9 us (41%)
  blocking collectives  65.1 us (31%)
  matrix products  15.4 us (7%)
  between operations  14.2 us (7%)
  other arithmetic  12.1 us (6%)
  starting transfers between devices  10 us (5%)
  local copies, waits for them, and re-layouts  6.42 us (3%)
    all_gather x1, waiting for transfers between devices, local(): gathered = lax.all_gather(features, ('tz', 'tc'), axis=1, tiled=True)  43.2 us
    reduce_scatter x1, waiting for transfers between devices, local(): lax.psum_scatter(partials, ('tz', 'tc'), scatter_dimension=1, tiled=True)  26.2 us
    all_to_all x1, blocking collectives, local(): blocks = lax.all_to_all(copies, ('vy', 'vx'), 0, 0, tiled=True)  21.4 us
    psum x1, blocking collectives, local(): lax.psum(lax.psum(lax.psum(local_stats, 'tc'), 'tz'), 'vy')  17 us
    psum x1, blocking collectives, local(): lax.psum(lax.psum(local_stats, 'tc'), 'tz')  15.7 us
    all_to_all x1, waiting for transfers between devices, local(): lax.all_to_all(blocks, ('vy', 'vx'), 0, 0, tiled=True)  15.5 us
    all_to_all x1, starting transfers between devices, local(): lax.all_to_all(blocks, ('vy', 'vx'), 0, 0, tiled=True)  9.94 us
    psum x1, blocking collectives, local(): lax.psum(lax.psum(lax.psum(lax.psum(local_stats, 'tc'), 'tz'), 'vy'), 'vx')  8.58 us
  transfers between devices with their start and end apart: 3, of which 3 were waited for; matrix products, arithmetic and copies ran while one was open for 2% of the time, Pallas kernels for 0%

profile of v5, /device:TPU:2, one launch (start us, length us, event | category | flops | bytes accessed | tf_op | source)
XLA Modules:
  0.0 208.2 jit_solution(17981607957040771834)
XLA Ops:
  7.2 0.8 pad_maximum_fusion.1
  8.1 21.4 %all_to_all.10 = bf16[32,2,16,72]{3,2,1,0:T(8,128)(2,1)S(1)} all-to-all(bf16[32,2,16,72]{3,2,1,0:T(8,128)(2,1)S(1)} %broadcast_in_dim.2), channel_id=1, replica_groups=mesh['tz'=8,'tc'=2,'vy'=8,'vx'=4] {'vy','vx'}, dimensions={0} | all-to-all | bytes 294912 | tf_op jit(solution)/shard_map/all_to_all | solution.py:17
  29.6 1.0 reshape.44
  30.7 43.2 %all-gather.2.cloned.1.call-done = bf16[2,256,2304]{2,1,0:T(8,128)(2,1)} async-done(((bf16[2,16,2304]{2,1,0:T(8,128)(2,1)}), bf16[2,256,2304]{2,1,0:T(8,128)(2,1)}) %all-gather.2.cloned.1.call-update) | async-done | bytes 2359312 | tf_op jit(solution)/shard_map/all_gather | solution.py:19
  73.9 2.0 fusion.6
  75.9 0.6 fusion.7
  76.5 0.6 fusion.5
  77.4 4.1 %fusion.3 = f32[2,256,2304]{2,1,0:T(8,128)S(1)} fusion(bf16[2304,256]{1,0:T(8,128)(2,1)S(1)} %copy-done.4, f32[1,256,256]{1,2,0:T(8,128)S(1)} %get-tuple-element.17, f32[1,256,256]{1,2,0:T(8,128)S(1)} %get-tuple-element.18), kind=kOutput, calls=%fused_computation.9 | convolution fusion | flops 3624009728 | bytes 6422528 | tf_op jit(solution)/shard_map/dot_general | solution.py:39
  81.5 5.9 %fusion.1 = f32[3,256,2304]{2,1,0:T(8,128)S(1)} fusion(bf16[2304,256]{1,0:T(8,128)(2,1)S(1)} %copy-done, f32[1,256,256]{1,2,0:T(8,128)S(1)} %get-tuple-element.14, f32[1,256,256]{1,2,0:T(8,128)S(1)} %get-tuple-element.18, f32[1,256,256]{1,2,0:T(8,128)S(1)} %get-tuple-element.13), kind=kOutput, calls=%fused_computation.7 | convolution fusion | flops 5436211200 | bytes 9043968 | tf_op jit(solution)/shard_map/dot_general | solution.py:43
  87.4 2.3 %slice_add_fusion.1 = (f32[1,256,2304]{2,1,0:T(8,128)S(1)}, f32[1,256,2304]{2,1,0:T(8,128)S(1)}, f32[1,256,2304]{2,1,0:T(8,128)}) fusion(f32[3,256,2304]{2,1,0:T(8,128)S(1)} %fusion.1, f32[2,256,2304]{2,1,0:T(8,128)S(1)} %fusion.3), kind=kLoop, calls=%fused_computation.3 | loop fusion | flops 1179648 | bytes 18874368 | tf_op jit(solution)/shard_map/add | solution.py:47
  89.7 5.1 %pad_maximum_fusion = f32[3,256,2304]{2,1,0:T(8,128)} fusion(f32[1,256,2304]{2,1,0:T(8,128)S(1)} %get-tuple-element.11, f32[1,256,2304]{2,1,0:T(8,128)} %get-tuple-element.12, f32[1,256,2304]{2,1,0:T(8,128)S(1)} %get-tuple-element.10), kind=kLoop, calls=%fused_computation | loop fusion | flops 3538944 | bytes 14155776 | tf_op jit(solution)/shard_map/stack | solution.py:47
  94.8 2.5 %psum.28 = f32[2,256]{1,0:T(2,128)S(1)} all-reduce(f32[2,256]{1,0:T(2,128)S(1)} %pad_maximum_fusion.2), channel_id=1, replica_groups=mesh['tz'=8,'tc'=2,'vy'=8,'vx'=4] {'tc'}, use_global_device_ids=true, to_apply=%region_2.0 | all-reduce | flops 512 | bytes 4096 | tf_op jit(solution)/shard_map/psum | solution.py:52
  97.3 15.7 %psum.29 = f32[2,256]{1,0:T(2,128)S(1)} all-reduce(f32[2,256]{1,0:T(2,128)S(1)} %psum.28), channel_id=1, replica_groups=mesh['tz'=8,'tc'=2,'vy'=8,'vx'=4] {'tz'}, use_global_device_ids=true, to_apply=%region_3.0 | all-reduce | flops 512 | bytes 4096 | tf_op jit(solution)/shard_map/psum | solution.py:52
  113.0 17.0 %psum.30 = f32[2,256]{1,0:T(2,128)S(1)} all-reduce(f32[2,256]{1,0:T(2,128)S(1)} %psum.29), channel_id=1, replica_groups=mesh['tz'=8,'tc'=2,'vy'=8,'vx'=4] {'vy'}, use_global_device_ids=true, to_apply=%region_4.0 | all-reduce | flops 512 | bytes 4096 | tf_op jit(solution)/shard_map/psum | solution.py:52
  130.0 8.6 %psum.31 = f32[2,256]{1,0:T(2,128)S(1)} all-reduce(f32[2,256]{1,0:T(2,128)S(1)} %psum.30), channel_id=1, replica_groups=mesh['tz'=8,'tc'=2,'vy'=8,'vx'=4] {'vx'}, use_global_device_ids=true, to_apply=%region_5.0 | all-reduce | flops 512 | bytes 4096 | tf_op jit(solution)/shard_map/psum | solution.py:52
  138.6 26.2 %reduce-scatter.2.cloned.1.call-done = f32[3,16,2304]{2,1,0:T(8,128)} async-done(((f32[3,256,2304]{2,1,0:T(8,128)}), f32[3,16,2304]{2,1,0:T(8,128)}) %reduce-scatter.2.cloned.1.call-update) | async-done | bytes 442384 | tf_op jit(solution)/shard_map/reduce_scatter | solution.py:51
  164.8 2.7 %reshape.45 = f32[3,16,32,72]{3,2,1,0:T(8,128)} reshape(f32[3,16,2304]{2,1,0:T(8,128)} %reduce-scatter.2.cloned.1.call-done) | data formatting | bytes 884736 | tf_op jit(solution)/shard_map/reshape | solution.py:54
  167.5 2.5 %copy.19 = f32[3,16,32,72]{3,1,0,2:T(8,128)} copy(f32[3,16,32,72]{3,2,1,0:T(8,128)} %reshape.45) | data formatting | bytes 884736 | tf_op jit(solution)/shard_map/reshape | solution.py:54
  170.0 9.9 %all-to-all-start.1 = ((f32[32,3,16,72]{3,2,1,0:T(8,128)}), f32[32,3,16,72]{3,2,1,0:T(8,128)}, u32[]{:S(2)}, u32[]{:S(2)}) async-start(f32[32,3,16,72]{3,2,1,0:T(8,128)} %bitcast.66), calls=%async_computation.2 | async-start | bytes 1572864 | tf_op jit(solution)/shard_map/all_to_all | solution.py:55
  180.5 1.2 fusion.26
  181.8 2.2 %convolution_bitcast_fusion = f32[2304,256]{1,0:T(8,128)} fusion(bf16[2,256,2304]{2,1,0:T(8,128)(2,1)S(1)} %copy-done.2, bf16[1,256,256]{1,2,0:T(8,128)(2,1)S(1)} %get-tuple-element.16, bf16[1,256,256]{1,2,0:T(8,128)(2,1)S(1)} %get-tuple-element.15), kind=kOutput, calls=%fused_computation.1 | convolution fusion | flops 604110848 | bytes 4980736 | tf_op jit(solution)/shard_map/krd,krv->dv/dot_general | solution.py:67
  184.0 15.5 %all-to-all-done.1 = f32[32,3,16,72]{3,2,1,0:T(8,128)} async-done(((f32[32,3,16,72]{3,2,1,0:T(8,128)}), f32[32,3,16,72]{3,2,1,0:T(8,128)}, u32[]{:S(2)}, u32[]{:S(2)}) %all-to-all-start.1) | async-done | bytes 442400 | tf_op jit(solution)/shard_map/all_to_all | solution.py:55
  199.5 1.2 reduce_sum.29
  200.7 0.7 fusion.27
  (28 shorter events, 1.1 us)
Async XLA Ops:
  7.2 66.7 %copy-start = (bf16[2304,256]{1,0:T(8,128)(2,1)S(1)}, bf16[2304,256]{1,0:T(8,128)(2,1)}, u32[]{:S(2)}) copy-start(bf16[2304,256]{1,0:T(8,128)(2,1)} %param.6) | copy-start | bytes 3538948
  7.2 66.7 %all-gather.2.cloned.1.call-start = ((), (), s32[]{:S(2)}) async-start(), calls=%async_computation.3 | async-start | bytes 2506752 | tf_op jit(solution)/shard_map/all_gather | solution.py:19
  8.0 67.9 %copy-start.4 = (bf16[2304,256]{1,0:T(8,128)(2,1)S(1)}, bf16[2304,256]{1,0:T(8,128)(2,1)}, u32[]{:S(2)}) copy-start(bf16[2304,256]{1,0:T(8,128)(2,1)} %param.9) | copy-start | bytes 3538948
  30.6 134.2 %reduce-scatter.2.cloned.1.call-start = ((), (), s32[]{:S(2)}) async-start(), calls=%async_computation.4 | async-start | bytes 7520256 | tf_op jit(solution)/shard_map/reduce_scatter | solution.py:51
  73.9 2.0 copy-start.1
  75.9 1.2 copy-start.5
  75.9 1.2 copy-start.6
  77.2 4.3 %copy-start.3 = (f32[256,256]{0,1:T(8,128)}, f32[256,256]{0,1:T(8,128)S(1)}, u32[]{:S(2)}) copy-start(f32[256,256]{0,1:T(8,128)S(1)} %fusion.5) | copy-start | bytes 786436
  138.6 43.2 %copy-start.2 = (bf16[2,256,2304]{2,1,0:T(8,128)(2,1)S(1)}, bf16[2,256,2304]{2,1,0:T(8,128)(2,1)}, u32[]{:S(2)}) copy-start(bf16[2,256,2304]{2,1,0:T(8,128)(2,1)} %all-gather.2.cloned.1.call-done) | copy-start | bytes 7077892
  170.0 29.5 %all-to-all-start.1 = ((f32[32,3,16,72]{3,2,1,0:T(8,128)}), f32[32,3,16,72]{3,2,1,0:T(8,128)}, u32[]{:S(2)}, u32[]{:S(2)}) async-start(f32[32,3,16,72]{3,2,1,0:T(8,128)} %bitcast.66), calls=%async_computation.2 | async-start | bytes 1572864 | tf_op jit(solution)/shard_map/all_to_all | solution.py:55
  181.8 18.9 %copy-start.7 = (f32[16]{0:T(128)S(1)}, f32[16]{0:T(128)}, u32[]{:S(2)}) copy-start(f32[16]{0:T(128)} %get-tuple-element.20) | copy-start | bytes 196
Sparse Core Ops, SparseCore 0:
  30.7 43.1 all-gather.1
  94.9 69.7 reduce-scatter.1

commit v6 on v4

--- a/solution.py
+++ b/solution.py
@@ -35,7 +35,7 @@
 
     weighted_slope = exponent * cap_slope
     weighted_tan = exponent * (cap_slope * cap_tangent + slope_tan)
-    hi = lax.Precision.HIGHEST
+    hi = lax.Precision.HIGH
     by_probe = lax.dot_general(
         jnp.stack([weighted_slope, onehot * cap_slope]), probe_head.astype(jnp.float32),
         (((2,), (1,)), ((), ())), precision=hi, preferred_element_type=jnp.float32,

time: 209 us -> 205 us (0.981)
  matrix products: 15.4 us -> 12.1 us
where the time goes in v6:
time: 205 us
  waiting for transfers between devices  77.8 us (38%)
  blocking collectives  72.2 us (35%)
  between operations  14.2 us (7%)
  matrix products  12.1 us (6%)
  other arithmetic  12 us (6%)
  starting transfers between devices  9.91 us (5%)
  local copies, waits for them, and re-layouts  6.41 us (3%)
    psum x3, blocking collectives, local(): stats = lax.psum(lax.psum(lax.psum(local_stats, 'tok'), 'vy'), 'vx')  50.8 us
    all_gather x1, waiting for transfers between devices, local(): gathered = lax.all_gather(features, 'tok', axis=1, tiled=True)  43.2 us
    all_to_all x1, blocking collectives, local(): blocks = lax.all_to_all(copies, ('vy', 'vx'), 0, 0, tiled=True)  21.4 us
    reduce_scatter x1, waiting for transfers between devices, local(): summed = lax.psum_scatter(partials, 'tok', scatter_dimension=1, tiled=True)  19.3 us
    all_to_all x1, waiting for transfers between devices, local(): lax.all_to_all(blocks, ('vy', 'vx'), 0, 0, tiled=True)  15.3 us
    all_to_all x1, starting transfers between devices, local(): lax.all_to_all(blocks, ('vy', 'vx'), 0, 0, tiled=True)  9.83 us
    reshape x2, local copies, waits for them, and re-layouts, local(): summed.reshape(kinds, rows, voc_count, width // voc_count)  5.19 us
    another operation x1, other arithmetic, local(): jnp.stack([by_probe[0] + by_head[0], by_head[1], by_probe[1] + by_head[2]])  5.14 us
  transfers between devices with their start and end apart: 3, of which 3 were waited for; matrix products, arithmetic and copies ran while one was open for 2% of the time, Pallas kernels for 0%

profile of v6, /device:TPU:2, one launch (start us, length us, event | category | flops | bytes accessed | tf_op | source)
XLA Modules:
  0.0 204.7 jit_solution(5712569975829166852)
XLA Ops:
  7.2 0.8 pad_maximum_fusion.1
  8.1 21.4 %all_to_all.10 = bf16[32,2,16,72]{3,2,1,0:T(8,128)(2,1)S(1)} all-to-all(bf16[32,2,16,72]{3,2,1,0:T(8,128)(2,1)S(1)} %broadcast_in_dim.2), channel_id=1, replica_groups=mesh['tok'=16,'vy'=8,'vx'=4] {'vy','vx'}, dimensions={0} | all-to-all | bytes 294912 | tf_op jit(solution)/shard_map/all_to_all | solution.py:17
  29.6 1.0 reshape.44
  30.7 43.2 %all-gather.2.cloned.1.call-done = bf16[2,256,2304]{2,1,0:T(8,128)(2,1)} async-done(((bf16[2,16,2304]{2,1,0:T(8,128)(2,1)}), bf16[2,256,2304]{2,1,0:T(8,128)(2,1)}) %all-gather.2.cloned.1.call-update) | async-done | bytes 2359312 | tf_op jit(solution)/shard_map/all_gather | solution.py:19
  73.9 2.0 fusion.6
  75.9 0.6 fusion.7
  76.5 0.6 fusion.5
  77.4 2.7 %fusion.3 = f32[2,256,2304]{2,1,0:T(8,128)S(1)} fusion(bf16[2304,256]{1,0:T(8,128)(2,1)S(1)} %copy-done.4, f32[1,256,256]{1,2,0:T(8,128)S(1)} %get-tuple-element.17, f32[1,256,256]{1,2,0:T(8,128)S(1)} %get-tuple-element.18), kind=kOutput, calls=%fused_computation.9 | convolution fusion | flops 1812070400 | bytes 6422528 | tf_op jit(solution)/shard_map/dot_general | solution.py:39
  80.1 4.0 %fusion.1 = f32[3,256,2304]{2,1,0:T(8,128)S(1)} fusion(bf16[2304,256]{1,0:T(8,128)(2,1)S(1)} %copy-done, f32[1,256,256]{1,2,0:T(8,128)S(1)} %get-tuple-element.14, f32[1,256,256]{1,2,0:T(8,128)S(1)} %get-tuple-element.18, f32[1,256,256]{1,2,0:T(8,128)S(1)} %get-tuple-element.13), kind=kOutput, calls=%fused_computation.7 | convolution fusion | flops 2718302208 | bytes 9043968 | tf_op jit(solution)/shard_map/dot_general | solution.py:43
  84.1 2.1 %slice_add_fusion.1 = (f32[1,256,2304]{2,1,0:T(8,128)S(1)}, f32[1,256,2304]{2,1,0:T(8,128)S(1)}, f32[1,256,2304]{2,1,0:T(8,128)}) fusion(f32[3,256,2304]{2,1,0:T(8,128)S(1)} %fusion.1, f32[2,256,2304]{2,1,0:T(8,128)S(1)} %fusion.3), kind=kLoop, calls=%fused_computation.3 | loop fusion | flops 1179648 | bytes 18874368 | tf_op jit(solution)/shard_map/add | solution.py:47
  86.2 5.1 %pad_maximum_fusion = f32[3,256,2304]{2,1,0:T(8,128)} fusion(f32[1,256,2304]{2,1,0:T(8,128)S(1)} %get-tuple-element.11, f32[1,256,2304]{2,1,0:T(8,128)} %get-tuple-element.12, f32[1,256,2304]{2,1,0:T(8,128)S(1)} %get-tuple-element.10), kind=kLoop, calls=%fused_computation | loop fusion | flops 3538944 | bytes 14155776 | tf_op jit(solution)/shard_map/stack | solution.py:47
  91.4 25.1 %psum.21 = f32[2,256]{1,0:T(2,128)S(1)} all-reduce(f32[2,256]{1,0:T(2,128)S(1)} %pad_maximum_fusion.2), channel_id=1, replica_groups=mesh['tok'=16,'vy'=8,'vx'=4] {'tok'}, use_global_device_ids=true, to_apply=%region_2.0 | all-reduce | flops 512 | bytes 4096 | tf_op jit(solution)/shard_map/psum | solution.py:52
  116.5 16.9 %psum.22 = f32[2,256]{1,0:T(2,128)S(1)} all-reduce(f32[2,256]{1,0:T(2,128)S(1)} %psum.21), channel_id=1, replica_groups=mesh['tok'=16,'vy'=8,'vx'=4] {'vy'}, use_global_device_ids=true, to_apply=%region_3.0 | all-reduce | flops 512 | bytes 4096 | tf_op jit(solution)/shard_map/psum | solution.py:52
  133.4 8.8 %psum.23 = f32[2,256]{1,0:T(2,128)S(1)} all-reduce(f32[2,256]{1,0:T(2,128)S(1)} %psum.22), channel_id=1, replica_groups=mesh['tok'=16,'vy'=8,'vx'=4] {'vx'}, use_global_device_ids=true, to_apply=%region_4.0 | all-reduce | flops 512 | bytes 4096 | tf_op jit(solution)/shard_map/psum | solution.py:52
  142.2 19.3 %reduce-scatter.2.cloned.1.call-done = f32[3,16,2304]{2,1,0:T(8,128)} async-done(((f32[3,256,2304]{2,1,0:T(8,128)}), f32[3,16,2304]{2,1,0:T(8,128)}) %reduce-scatter.2.cloned.1.call-update) | async-done | bytes 442384 | tf_op jit(solution)/shard_map/reduce_scatter | solution.py:51
  161.5 2.7 %reshape.45 = f32[3,16,32,72]{3,2,1,0:T(8,128)} reshape(f32[3,16,2304]{2,1,0:T(8,128)} %reduce-scatter.2.cloned.1.call-done) | data formatting | bytes 884736 | tf_op jit(solution)/shard_map/reshape | solution.py:54
  164.2 2.5 %copy.19 = f32[3,16,32,72]{3,1,0,2:T(8,128)} copy(f32[3,16,32,72]{3,2,1,0:T(8,128)} %reshape.45) | data formatting | bytes 884736 | tf_op jit(solution)/shard_map/reshape | solution.py:54
  166.7 9.8 %all-to-all-start.1 = ((f32[32,3,16,72]{3,2,1,0:T(8,128)}), f32[32,3,16,72]{3,2,1,0:T(8,128)}, u32[]{:S(2)}, u32[]{:S(2)}) async-start(f32[32,3,16,72]{3,2,1,0:T(8,128)} %bitcast.66), calls=%async_computation.2 | async-start | bytes 1572864 | tf_op jit(solution)/shard_map/all_to_all | solution.py:55
  176.5 0.6 bitcast_divide_fusion.1
  177.1 1.2 fusion.26
  178.4 2.2 %convolution_bitcast_fusion = f32[2304,256]{1,0:T(8,128)} fusion(bf16[2,256,2304]{2,1,0:T(8,128)(2,1)S(1)} %copy-done.2, bf16[1,256,256]{1,2,0:T(8,128)(2,1)S(1)} %get-tuple-element.16, bf16[1,256,256]{1,2,0:T(8,128)(2,1)S(1)} %get-tuple-element.15), kind=kOutput, calls=%fused_computation.1 | convolution fusion | flops 604110848 | bytes 4980736 | tf_op jit(solution)/shard_map/krd,krv->dv/dot_general | solution.py:67
  180.6 15.3 %all-to-all-done.1 = f32[32,3,16,72]{3,2,1,0:T(8,128)} async-done(((f32[32,3,16,72]{3,2,1,0:T(8,128)}), f32[32,3,16,72]{3,2,1,0:T(8,128)}, u32[]{:S(2)}, u32[]{:S(2)}) %all-to-all-start.1) | async-done | bytes 442400 | tf_op jit(solution)/shard_map/all_to_all | solution.py:55
  196.0 1.2 reduce_sum.29
  197.2 0.7 fusion.27
  (27 shorter events, 0.5 us)
Async XLA Ops:
  7.2 66.7 %copy-start = (bf16[2304,256]{1,0:T(8,128)(2,1)S(1)}, bf16[2304,256]{1,0:T(8,128)(2,1)}, u32[]{:S(2)}) copy-start(bf16[2304,256]{1,0:T(8,128)(2,1)} %param.6) | copy-start | bytes 3538948
  7.2 66.7 %all-gather.2.cloned.1.call-start = ((), (), s32[]{:S(2)}) async-start(), calls=%async_computation.3 | async-start | bytes 2506752 | tf_op jit(solution)/shard_map/all_gather | solution.py:19
  8.0 67.9 %copy-start.4 = (bf16[2304,256]{1,0:T(8,128)(2,1)S(1)}, bf16[2304,256]{1,0:T(8,128)(2,1)}, u32[]{:S(2)}) copy-start(bf16[2304,256]{1,0:T(8,128)(2,1)} %param.9) | copy-start | bytes 3538948
  30.6 130.9 %reduce-scatter.2.cloned.1.call-start = ((), (), s32[]{:S(2)}) async-start(), calls=%async_computation.4 | async-start | bytes 7520256 | tf_op jit(solution)/shard_map/reduce_scatter | solution.py:51
  73.9 2.0 copy-start.1
  75.9 1.2 copy-start.5
  75.9 1.2 copy-start.6
  77.2 3.0 %copy-start.3 = (f32[256,256]{0,1:T(8,128)}, f32[256,256]{0,1:T(8,128)S(1)}, u32[]{:S(2)}) copy-start(f32[256,256]{0,1:T(8,128)S(1)} %fusion.5) | copy-start | bytes 786436
  142.2 36.2 %copy-start.2 = (bf16[2,256,2304]{2,1,0:T(8,128)(2,1)S(1)}, bf16[2,256,2304]{2,1,0:T(8,128)(2,1)}, u32[]{:S(2)}) copy-start(bf16[2,256,2304]{2,1,0:T(8,128)(2,1)} %all-gather.2.cloned.1.call-done) | copy-start | bytes 7077892
  166.7 29.3 %all-to-all-start.1 = ((f32[32,3,16,72]{3,2,1,0:T(8,128)}), f32[32,3,16,72]{3,2,1,0:T(8,128)}, u32[]{:S(2)}, u32[]{:S(2)}) async-start(f32[32,3,16,72]{3,2,1,0:T(8,128)} %bitcast.66), calls=%async_computation.2 | async-start | bytes 1572864 | tf_op jit(solution)/shard_map/all_to_all | solution.py:55
  178.4 18.8 %copy-start.7 = (f32[16]{0:T(128)S(1)}, f32[16]{0:T(128)}, u32[]{:S(2)}) copy-start(f32[16]{0:T(128)} %get-tuple-element.20) | copy-start | bytes 196
Sparse Core Ops, SparseCore 0:
  30.7 43.1 all-gather.1
  91.5 69.9 reduce-scatter.1
